TPU v7x, 32 devices: a whole 2x2x4 slice. The times are simulated.
32 devices in a mesh: seq: 4 (over y, x), fsdp: 8 (over z, core).
Axes of the slice: x: 2, y: 2, z: 4, core: 2. Of those that a mesh axis runs over, the one named last changes fastest.
Arguments:
- tokens: bfloat16 [8, 1024, 1536], P('fsdp', 'seq'), may hold values from -6 to 6
- mixing_weight: bfloat16 [1536, 2560], P(('seq', 'fsdp')), may hold values from -0.21875 to 0.21875
- output_weight: bfloat16 [1536, 1536], P(('seq', 'fsdp')), may hold values from -0.625 to 0.625
- norm_gains: bfloat16 [1536, 2], P(('seq', 'fsdp')), may hold values from 0.099609375 to 1.8984375
- expert_gate: bfloat16 [1536, 40, 512], P('fsdp', 'seq'), may hold values from -0.15625 to 0.15625
- expert_up: bfloat16 [1536, 40, 512], P('fsdp', 'seq'), may hold values from -0.15625 to 0.15625
- expert_down: bfloat16 [1536, 40, 512], P('fsdp', 'seq'), may hold values from -1.25 to 1.25
- gate_logits: float32 [8, 1024, 8], P('fsdp'), may hold values from -3 to 3
- routes: int32 [8, 1024, 8], P('fsdp'), may hold values from 0 to 39, all different within a row
- fill_order: int32 [8, 1024], P('fsdp'), may hold values from 0 to 1023, each once within a row
- cotangent: bfloat16 [8, 1024, 1536], P('fsdp', 'seq'), may hold values from -6 to 6
Outputs:
- layer_output: bfloat16 [8, 1024, 1536], P('fsdp', 'seq')
- tokens_gradient: float32 [8, 1024, 1536], P('fsdp', 'seq')
- mixing_gradient: float32 [1536, 2560], P(('seq', 'fsdp'))
- output_gradient: float32 [1536, 1536], P(('seq', 'fsdp'))
- gains_gradient: float32 [1536, 2], P(('seq', 'fsdp'))
- gate_gradient: float32 [1536, 40, 512], P('fsdp', 'seq')
- up_gradient: float32 [1536, 40, 512], P('fsdp', 'seq')
- down_gradient: float32 [1536, 40, 512], P('fsdp', 'seq')
- logits_gradient: float32 [8, 1024, 8], P('fsdp', 'seq')
Inputs may be any that keep to these rules, and one draw needn't show every extreme that they name: `routes`: each token names 8 different experts. `fill_order`: each sequence's row holds each token index of that sequence once.
All inputs are finite; a program needn't handle non-finite values.
Results may differ from a plain program's by a relative error of at most 0.017.
The roundings to bfloat16 on the way count: a program that leaves them out, or rounds other values in their place, can miss the bound.
Values may be sent and summed in bfloat16 or wider, within the bound.
A program may use at most 256 MiB of HBM per device.

v0:
```python
import math
import jax
import jax.numpy as jnp
from jax import lax
from jax.sharding import PartitionSpec as P

D = 1536
HEADS = 24
KV_HEADS = 8
HEAD_DIM = 64
FF = 512
EXPERTS = 40
TOP = 8
QBLK = 512
epsilon = 1e-05
rope_base = 10000.0


def norm_apply(values, gain_row):
    return (
        values * lax.rsqrt(jnp.mean(values * values, axis=-1, keepdims=True) + epsilon) * gain_row
    )


def rotary_tables(positions):
    half_width = HEAD_DIM // 2
    frequency = rope_base ** (-2.0 * jnp.arange(half_width, dtype=jnp.float32) / HEAD_DIM)
    angles = positions.astype(jnp.float32)[:, None] * frequency[None, :]
    cos_table = jnp.cos(angles)
    sin_table = jnp.sin(angles)
    return (jnp.concatenate([cos_table, cos_table], 1), jnp.concatenate([sin_table, sin_table], 1))


def rotate(values, cos_table, sin_table):
    half_width = values.shape[-1] // 2
    turned = jnp.concatenate([-values[..., half_width:], values[..., :half_width]], -1)
    return values * cos_table[:, None, :] + turned * sin_table[:, None, :]


def softmax_last(logit_rows):
    row_max = jnp.max(logit_rows, axis=-1, keepdims=True)
    exponent = jnp.exp(logit_rows - row_max)
    return exponent / jnp.sum(exponent, axis=-1, keepdims=True)


def build_slots(route_rows, order_rows, expert_ids, capacity):
    length = route_rows.shape[0]
    chosen = route_rows[:, :, None] == expert_ids[None, None, :]
    hit_count = jnp.sum(chosen.astype(jnp.int32), axis=1)
    ordered = hit_count[order_rows]
    before = jnp.cumsum(ordered, axis=0) - ordered
    slot_rank = jnp.zeros_like(before).at[order_rows].set(before)
    kept_mask = (hit_count > 0) & (slot_rank < capacity)
    slot_place = jnp.where(kept_mask, slot_rank, capacity)
    expert_cols = jnp.broadcast_to(
        jnp.arange(expert_ids.shape[0], dtype=jnp.int32)[None, :], slot_place.shape
    )
    token_ids = jnp.broadcast_to(jnp.arange(length, dtype=jnp.int32)[:, None], slot_place.shape)
    table_full = jnp.full((expert_ids.shape[0], capacity + 1), length, jnp.int32)
    table_full = table_full.at[expert_cols, slot_place].set(token_ids)
    return (chosen, table_full[:, :capacity])


def local(
    tokens,
    mixing_weight,
    output_weight,
    norm_gains,
    expert_gate,
    expert_up,
    expert_down,
    gate_logits,
    routes,
    fill_order,
    cotangent,
):
    single = jnp.float32
    narrow = jnp.bfloat16
    groups = lax.axis_size("seq")
    column = lax.axis_index("seq")
    tok_rows = tokens.shape[1]
    seq_len = tok_rows * groups
    capacity = (seq_len * TOP + EXPERTS - 1) // EXPERTS
    local_count = expert_gate.shape[1]
    query_width = HEADS * HEAD_DIM
    key_width = KV_HEADS * HEAD_DIM
    mixing_width = query_width + 2 * key_width
    score_scale = 1.0 / math.sqrt(HEAD_DIM)
    group_size = HEADS // KV_HEADS
    inputs = tokens[0].astype(single)
    mixing_full, exit_full, gains_full = (
        lax.all_gather(mixing_weight, ("seq", "fsdp"), axis=0, tiled=True),
        lax.all_gather(output_weight, ("seq", "fsdp"), axis=0, tiled=True),
        lax.all_gather(norm_gains, ("seq", "fsdp"), axis=0, tiled=True),
    )
    gains_float = gains_full.astype(single)
    normed = norm_apply(inputs, gains_float[:, 0])
    normed_low = normed.astype(narrow)
    projected = jnp.dot(normed_low, mixing_full, preferred_element_type=single)
    positions = column * tok_rows + jnp.arange(tok_rows, dtype=jnp.int32)
    cos_table, sin_table = rotary_tables(positions)
    query_raw = projected[:, :query_width].reshape(tok_rows, HEADS, HEAD_DIM)
    key_raw = projected[:, query_width : query_width + key_width].reshape(
        tok_rows, KV_HEADS, HEAD_DIM
    )
    query_send = (
        rotate(query_raw, cos_table, sin_table).reshape(tok_rows, query_width).astype(narrow)
    )
    key_send = rotate(key_raw, cos_table, sin_table).reshape(tok_rows, key_width).astype(narrow)
    value_send = projected[:, query_width + key_width :].astype(narrow)
    query_heads, key_heads, value_heads = (
        lax.all_to_all(query_send, "seq", split_axis=1, concat_axis=0, tiled=True),
        lax.all_to_all(key_send, "seq", split_axis=1, concat_axis=0, tiled=True),
        lax.all_to_all(value_send, "seq", split_axis=1, concat_axis=0, tiled=True),
    )
    local_kv = key_heads.shape[1] // HEAD_DIM
    blocks = seq_len // QBLK
    query_blocks = query_heads.reshape(blocks, QBLK, local_kv, group_size, HEAD_DIM)
    key_heads = key_heads.reshape(seq_len, local_kv, HEAD_DIM)
    value_heads = value_heads.reshape(seq_len, local_kv, HEAD_DIM)
    starts = jnp.arange(blocks, dtype=jnp.int32) * QBLK
    key_pos = jnp.arange(seq_len, dtype=jnp.int32)

    def block_scores(row_block, first_row):
        scores = (
            jnp.einsum("bkgd,tkd->kgbt", row_block, key_heads, preferred_element_type=single)
            * score_scale
        )
        allowed = (first_row + jnp.arange(QBLK, dtype=jnp.int32))[:, None] >= key_pos[None, :]
        return jnp.where(allowed, scores, -jnp.inf)

    def attend(block_items):
        row_block, first_row = block_items
        scores = block_scores(row_block, first_row)
        row_max = jnp.max(scores, axis=-1, keepdims=True)
        exponent = jnp.exp(scores - row_max)
        row_total = jnp.sum(exponent, axis=-1, keepdims=True)
        soft_weights = (exponent / row_total).astype(narrow)
        attended = jnp.einsum(
            "kgbt,tkd->bkgd", soft_weights, value_heads, preferred_element_type=single
        )
        return (attended.astype(narrow), (row_max + jnp.log(row_total))[..., 0])

    attended_blocks, log_totals = lax.map(attend, (query_blocks, starts))
    attended_heads = attended_blocks.reshape(seq_len, -1)
    attn_rows = lax.all_to_all(attended_heads, "seq", split_axis=0, concat_axis=1, tiled=True)
    attn_out = lax.dot_general(
        attn_rows, exit_full, (((1,), (1,)), ((), ())), preferred_element_type=single
    )
    hidden = inputs + attn_out
    normed_two = norm_apply(hidden, gains_float[:, 1])
    normed_two_low = normed_two.astype(narrow)
    seq_rows = lax.all_gather(normed_two_low, "seq", axis=0, tiled=True)
    expert_ids = column * local_count + jnp.arange(local_count, dtype=jnp.int32)
    gating = softmax_last(gate_logits[0])
    chosen, slot_table = build_slots(routes[0], fill_order[0], expert_ids, capacity)
    chosen_float = chosen.astype(single)
    token_weight = jnp.sum(gating[:, :, None] * chosen_float, axis=1)
    padded_weight = jnp.concatenate([token_weight, jnp.zeros((1, local_count), single)], 0)
    expert_cols = jnp.arange(local_count, dtype=jnp.int32)[:, None]
    slot_weight = padded_weight[slot_table, expert_cols]
    padded_rows = jnp.concatenate([seq_rows, jnp.zeros((1, D), narrow)], 0)
    slot_rows = padded_rows[slot_table]
    gate_full, up_full, down_full = (
        lax.all_gather(expert_gate, "fsdp", axis=0, tiled=True),
        lax.all_gather(expert_up, "fsdp", axis=0, tiled=True),
        lax.all_gather(expert_down, "fsdp", axis=0, tiled=True),
    )
    gate_pre = jnp.einsum("ecd,def->ecf", slot_rows, gate_full, preferred_element_type=single)
    up_pre = jnp.einsum("ecd,def->ecf", slot_rows, up_full, preferred_element_type=single)
    sigmoid_gate = jax.nn.sigmoid(gate_pre)
    mid_low = (gate_pre * sigmoid_gate * up_pre).astype(narrow)
    expert_out = jnp.einsum("ecf,def->ecd", mid_low, down_full, preferred_element_type=single)
    partial_sum = (
        jnp.zeros((seq_len + 1, D), single)
        .at[slot_table]
        .add(expert_out * slot_weight[:, :, None])[:seq_len]
    )
    moe_rows = lax.psum_scatter(
        partial_sum.astype(jnp.bfloat16), "seq", scatter_dimension=0, tiled=True
    ).astype(jnp.float32)
    layer_output = (hidden + moe_rows).astype(narrow)[None]
    cot_rows = lax.all_gather(cotangent[0], "seq", axis=0, tiled=True)
    padded_cot = jnp.concatenate([cot_rows, jnp.zeros((1, D), narrow)], 0)
    slot_cot = padded_cot[slot_table].astype(single)
    slot_weight_grad = jnp.sum(slot_cot * expert_out, axis=-1)
    out_low = (slot_cot * slot_weight[:, :, None]).astype(narrow)
    gate_full, up_full, down_full = (
        lax.all_gather(expert_gate, "fsdp", axis=0, tiled=True),
        lax.all_gather(expert_up, "fsdp", axis=0, tiled=True),
        lax.all_gather(expert_down, "fsdp", axis=0, tiled=True),
    )
    mid_grad = jnp.einsum("ecd,def->ecf", out_low, down_full, preferred_element_type=single)
    gate_grad_low = (
        mid_grad * up_pre * sigmoid_gate * (1.0 + gate_pre * (1.0 - sigmoid_gate))
    ).astype(narrow)
    up_grad_low = (mid_grad * gate_pre * sigmoid_gate).astype(narrow)
    row_grad = jnp.einsum("ecf,def->ecd", gate_grad_low, gate_full, preferred_element_type=single)
    row_grad = row_grad + jnp.einsum(
        "ecf,def->ecd", up_grad_low, up_full, preferred_element_type=single
    )
    normed_two_part = jnp.zeros((seq_len + 1, D), single).at[slot_table].add(row_grad)[:seq_len]
    weight_grad_tok = (
        jnp.zeros((seq_len + 1, local_count), single)
        .at[slot_table, expert_cols]
        .add(slot_weight_grad)[:seq_len]
    )
    route_grad = jnp.sum(weight_grad_tok[:, None, :] * chosen_float, axis=-1)
    logit_part = gating * (route_grad - jnp.sum(gating * route_grad, axis=-1, keepdims=True))
    normed_two_grad, logits_rows = (
        lax.psum_scatter(normed_two_part, "seq", scatter_dimension=0, tiled=True),
        lax.psum_scatter(logit_part, "seq", scatter_dimension=0, tiled=True),
    )
    gate_term = jnp.einsum("ecd,ecf->def", slot_rows, gate_grad_low, preferred_element_type=single)
    up_term = jnp.einsum("ecd,ecf->def", slot_rows, up_grad_low, preferred_element_type=single)
    down_term = jnp.einsum("ecd,ecf->def", out_low, mid_low, preferred_element_type=single)
    expert_total = lax.psum_scatter(
        jnp.concatenate([gate_term, up_term, down_term], 2).astype(jnp.bfloat16),
        "fsdp",
        scatter_dimension=0,
        tiled=True,
    ).astype(jnp.float32)
    unused, norm_two_back = jax.vjp(norm_apply, hidden, gains_float[:, 1])
    hidden_part, gain_two_grad = norm_two_back(normed_two_grad)
    hidden_grad = cotangent[0].astype(single) + hidden_part
    attn_grad_low = hidden_grad.astype(narrow)
    attended_grad = jnp.dot(attn_grad_low, exit_full, preferred_element_type=single).astype(narrow)
    grads_heads = lax.all_to_all(attended_grad, "seq", split_axis=1, concat_axis=0, tiled=True)
    grad_blocks = grads_heads.reshape(blocks, QBLK, local_kv, group_size, HEAD_DIM)

    def attend_back(carried, block_items):
        keys_sum, values_sum = carried
        row_block, grad_block, block_log, first_row = block_items
        scores = block_scores(row_block, first_row)
        soft_float = jnp.exp(scores - block_log[..., None])
        soft_weights = soft_float.astype(narrow)
        values_sum = values_sum + jnp.einsum(
            "kgbt,bkgd->tkd", soft_weights, grad_block, preferred_element_type=single
        )
        soft_grad = jnp.einsum(
            "bkgd,tkd->kgbt", grad_block, value_heads, preferred_element_type=single
        )
        row_delta = jnp.sum(soft_float * soft_grad, axis=-1, keepdims=True)
        scores_grad = (soft_float * (soft_grad - row_delta)).astype(narrow)
        query_grad = (
            jnp.einsum("kgbt,tkd->bkgd", scores_grad, key_heads, preferred_element_type=single)
            * score_scale
        )
        keys_sum = (
            keys_sum
            + jnp.einsum("kgbt,bkgd->tkd", scores_grad, row_block, preferred_element_type=single)
            * score_scale
        )
        return ((keys_sum, values_sum), query_grad.astype(narrow))

    zero_heads = jnp.zeros((seq_len, local_kv, HEAD_DIM), single)
    (keys_sum, values_sum), query_grads = lax.scan(
        attend_back, (zero_heads, zero_heads), (query_blocks, grad_blocks, log_totals, starts)
    )
    query_send_grad = query_grads.reshape(seq_len, -1)
    key_send_grad = keys_sum.reshape(seq_len, -1).astype(narrow)
    value_send_grad = values_sum.reshape(seq_len, -1).astype(narrow)
    query_back, key_back, value_back = (
        lax.all_to_all(query_send_grad, "seq", split_axis=0, concat_axis=1, tiled=True),
        lax.all_to_all(key_send_grad, "seq", split_axis=0, concat_axis=1, tiled=True),
        lax.all_to_all(value_send_grad, "seq", split_axis=0, concat_axis=1, tiled=True),
    )

    def turn_rows(entries):
        return rotate(entries, cos_table, sin_table)

    unused, query_turn_back = jax.vjp(turn_rows, query_raw)
    unused, key_turn_back = jax.vjp(turn_rows, key_raw)
    query_raw_grad = query_turn_back(query_back.astype(single).reshape(tok_rows, HEADS, HEAD_DIM))[
        0
    ]
    key_raw_grad = key_turn_back(key_back.astype(single).reshape(tok_rows, KV_HEADS, HEAD_DIM))[0]
    projected_grad = jnp.concatenate(
        [
            query_raw_grad.reshape(tok_rows, query_width).astype(narrow),
            key_raw_grad.reshape(tok_rows, key_width).astype(narrow),
            value_back,
        ],
        1,
    )
    normed_grad = lax.dot_general(
        projected_grad, mixing_full, (((1,), (1,)), ((), ())), preferred_element_type=single
    )
    unused, norm_one_back = jax.vjp(norm_apply, inputs, gains_float[:, 0])
    input_part, gain_one_grad = norm_one_back(normed_grad)
    tokens_gradient = (hidden_grad + input_part)[None]
    gains_term = jnp.stack([gain_one_grad, gain_two_grad], 1)
    mixing_term = lax.dot_general(
        normed_low, projected_grad, (((0,), (0,)), ((), ())), preferred_element_type=single
    )
    output_term = lax.dot_general(
        attn_grad_low, attn_rows, (((0,), (0,)), ((), ())), preferred_element_type=single
    )
    attn_total = lax.psum_scatter(
        jnp.concatenate([mixing_term, output_term, gains_term], 1),
        ("seq", "fsdp"),
        scatter_dimension=0,
        tiled=True,
    )
    mixing_gradient = attn_total[:, :mixing_width]
    output_gradient = attn_total[:, mixing_width : mixing_width + query_width]
    gains_gradient = attn_total[:, mixing_width + query_width :]
    gate_gradient = expert_total[:, :, :FF]
    up_gradient = expert_total[:, :, FF : 2 * FF]
    down_gradient = expert_total[:, :, 2 * FF :]
    return (
        layer_output,
        tokens_gradient,
        mixing_gradient,
        output_gradient,
        gains_gradient,
        gate_gradient,
        up_gradient,
        down_gradient,
        logits_rows[None],
    )


def solution(mesh):
    in_specs = (
        P("fsdp", "seq", None),
        P(("seq", "fsdp"), None),
        P(("seq", "fsdp"), None),
        P(("seq", "fsdp"), None),
        P("fsdp", "seq", None),
        P("fsdp", "seq", None),
        P("fsdp", "seq", None),
        P("fsdp", None, None),
        P("fsdp", None, None),
        P("fsdp", None),
        P("fsdp", "seq", None),
    )
    out_specs = (
        P("fsdp", "seq", None),
        P("fsdp", "seq", None),
        P(("seq", "fsdp"), None),
        P(("seq", "fsdp"), None),
        P(("seq", "fsdp"), None),
        P("fsdp", "seq", None),
        P("fsdp", "seq", None),
        P("fsdp", "seq", None),
        P("fsdp", "seq", None),
    )
    return jax.shard_map(local, mesh=mesh, in_specs=in_specs, out_specs=out_specs, check_vma=False)
```

profile of v0, /device:TPU:0, one launch (start us, length us, event | category | flops | bytes accessed | tf_op | source)
XLA Modules:
  0.0 1854.2 jit_solution(63584453304176128)
XLA Ops:
  8.7 43.3 %all-gather.1 = bf16[32,48,2]{1,2,0:T(2,128)(2,1)S(1)} all-gather(bf16[1,48,2]{1,2,0:T(2,128)(2,1)} %bitcast.352), channel_id=1, replica_groups=mesh['seq'=4,'fsdp'=8] {'seq','fsdp'}, dimensions={0}, use_global_device_ids=true | all-gather | bytes 6336 | tf_op jit(solution)/shard_map/all_gather | solution.py:94
  57.3 32.0 %all-gather.10.cloned.1.call-done = bf16[1536,2560]{1,0:T(8,128)(2,1)} async-done(((bf16[48,2560]{1,0:T(8,128)(2,1)}), bf16[1536,2560]{1,0:T(8,128)(2,1)}) %all-gather.10.cloned.1.call-update) | async-done | bytes 7864336 | tf_op jit(solution)/shard_map/all_gather | solution.py:92
  131.2 12.9 all-to-all-done
  147.4 23.8 %while.28 = (s32[]{:T(128)}, bf16[2,512,2,3,64]{1,4,3,2,0:T(8,128)(2,1)S(1)}, f32[2,2,3,512]{3,2,1,0:T(4,128)S(1)}, s32[2]{0:T(128)S(1)}, bf16[2,512,2,3,64]{1,4...) while((s32[]{:T(128)}, ...), condition=%wide.region_4.5_spmd.clone, body=%wide.region_1.4_spmd.clone.sunk | while | flops 843773440 | bytes 41279608 | solution.py:144
  180.1 12.1 all-to-all-done.3
  213.5 37.9 %scatter_custom_fusion.3 = s32[2060]{0:T(1024)S(1)} fusion(s32[10240]{0:T(1024)S(1)} %reshape.356, s32[10240]{0:T(1024)S(1)} %reshape.358, s32[]{:T(128)} %constant.52.clone.1), kind=kCustom, calls=%fused_computation.179 | custom fusion | bytes 8244
  263.3 11.4 reshape.378
  294.1 101.2 %all-gather.16.cloned.1.call-done = bf16[1536,10,512]{2,0,1:T(8,128)(2,1)} async-done(((bf16[192,10,512]{2,0,1:T(8,128)(2,1)}), bf16[1536,10,512]{2,0,1:T(8,128)(2,1)}) %all-gather.16.cloned.1.call-update) | async-done | bytes 15728656 | tf_op jit(solution)/shard_map/all_gather | solution.py:165
  395.3 13.3 fusion.103
  408.6 128.9 %all-gather.18.cloned.1.call-done = bf16[1536,10,512]{2,0,1:T(8,128)(2,1)} async-done(((bf16[192,10,512]{2,0,1:T(8,128)(2,1)}), bf16[1536,10,512]{2,0,1:T(8,128)(2,1)}) %all-gather.18.cloned.1.call-update) | async-done | bytes 15728656 | tf_op jit(solution)/shard_map/all_gather | solution.py:166
  537.5 15.1 multiply_convert_fusion.3
  552.6 127.2 %all-gather.20.cloned.1.call-done = bf16[1536,10,512]{2,0,1:T(8,128)(2,1)} async-done(((bf16[192,10,512]{2,0,1:T(8,128)(2,1)}), bf16[1536,10,512]{2,0,1:T(8,128)(2,1)}) %all-gather.20.cloned.1.call-update) | async-done | bytes 15728656 | tf_op jit(solution)/shard_map/all_gather | solution.py:167
  679.8 15.5 multiply_reduce_fusion
  695.4 16.0 scatter_custom_fusion.4
  712.6 19.8 %gather_fusion.2 = f32[2050]{0:T(1024)S(1)} fusion(f32[1025,10]{1,0:T(8,128)S(1)} %concatenate.44, s32[2050]{0:T(1024)S(1)} %reshape.318), kind=kCustom, calls=%fused_computation.2 | custom fusion | bytes 32800 | tf_op jit(solution)/shard_map/gather | solution.py:161
  732.5 15.0 multiply_convert_fusion.1
  747.5 12.8 fusion.104
  760.3 15.0 convolution_add_fusion
  775.3 12.5 reshape.352
  787.8 29.5 %scatter_custom_fusion.2 = f32[1025,1536]{1,0:T(8,128)} fusion(s32[2050]{0:T(1024)S(1)} %reshape.342, f32[2050,1536]{1,0:T(8,128)} %reshape.352, f32[]{:T(128)} %constant.30.clone.1), kind=kCustom, calls=%fused_computation.87 | custom fusion | flops 3148800 | bytes 6298112 | tf_op jit(solution)/shard_map/scatter-add | solution.py:202
  833.5 13.2 reshape.344
  846.7 29.4 %scatter_custom_fusion.1 = f32[1025,1536]{1,0:T(8,128)} fusion(s32[2050]{0:T(1024)S(1)} %reshape.342, f32[2050,1536]{1,0:T(8,128)} %reshape.344, f32[]{:T(128)} %constant.30.clone.1), kind=kCustom, calls=%fused_computation.89 | custom fusion | flops 3148800 | bytes 6298112 | tf_op jit(solution)/shard_map/scatter-add | solution.py:177
  894.3 45.2 %reduce-scatter.8.cloned.1.call-done = bf16[256,1536]{1,0:T(8,128)(2,1)} async-done(((bf16[1024,1536]{1,0:T(8,128)(2,1)}), bf16[256,1536]{1,0:T(8,128)(2,1)}) %reduce-scatter.8.cloned.1.call-update) | async-done | bytes 786448 | tf_op jit(solution)/shard_map/reduce_scatter | solution.py:179
  966.4 56.4 %while.29 = (s32[]{:T(128)}, f32[1024,2,64]{0,2,1:T(8,128)S(1)}, f32[1024,2,64]{0,2,1:T(8,128)}, bf16[2,512,2,3,64]{1,4,3,2,0:T(8,128)(2,1)}, bf16[2,512,2,3,64]...) while((s32[]{:T(128)}, f32[1024,2,64]{0,2,1:T(8,128)S(1)}, ...), condition=%wide.region_21.22_spmd.clone, body=%wide.region_19.21_spmd.clone.sunk | while | flops 2062022144 | bytes 184250800 | solution.py:257
  1076.1 27.7 %concatenate.48 = f32[1536,4098]{1,0:T(8,128)} concatenate(f32[1536,2560]{1,0:T(8,128)} %fusion.72, f32[1536,1536]{1,0:T(8,128)} %fusion.75, f32[1536,1]{1,0:T(8,128)S(1)} %stack.8, f32[1536,1]{1,0:T(8,128)S(1)} %copy-done.25), dimensions={1} | concatenate | bytes 50356224 | tf_op jit(solution)/shard_map/concatenate | solution.py:300
  1105.4 12.4 convert_bitcast_fusion.1
  1117.8 12.8 convert_bitcast_fusion.2
  1130.6 15.1 convert_bitcast_fusion
  1145.7 35.1 %pad_maximum_fusion = bf16[1536,10,1536]{0,2,1:T(8,128)(2,1)} fusion(bf16[1536,10,512]{0,2,1:T(8,128)(2,1)} %convert_bitcast_fusion, bf16[1536,10,512]{0,2,1:T(8,128)(2,1)} %convert_bitcast_fusion.1, bf16[1536,10,512]{0,2,1:T(8,128)(2,1)} %convert_bitcast_fusion.2), kind=kLoop, calls=%fused_computation.74 | loop fusion | flops 141557760 | bytes 94371840 | tf_op jit(solution)/shard_map/concatenate | solution.py:218
  1180.8 57.6 %copy.314 = bf16[1536,15360]{1,0:T(8,128)(2,1)} copy(bf16[1536,15360]{0,1:T(8,128)(2,1)} %bitcast.320) | data formatting | bytes 94371840
  1242.9 112.8 %reduce-scatter.12.cloned.1.call-done = f32[48,4098]{1,0:T(8,128)} async-done(((f32[1536,4098]{1,0:T(8,128)}), f32[48,4098]{1,0:T(8,128)}) %reduce-scatter.12.cloned.1.call-update) | async-done | bytes 786832 | tf_op jit(solution)/shard_map/reduce_scatter | solution.py:299
  1360.7 450.7 %reduce-scatter.16.cloned.1.call-done = bf16[192,15360]{1,0:T(8,128)(2,1)} async-done(((bf16[1536,15360]{1,0:T(8,128)(2,1)}), bf16[192,15360]{1,0:T(8,128)(2,1)}) %reduce-scatter.16.cloned.1.call-update) | async-done | bytes 5898256
  (378 shorter events, 354.4 us)
Async XLA Ops:
  7.2 49.8 %copy-start.17 = (bf16[1,256,1536]{2,1,0:T(8,128)(2,1)S(1)}, bf16[1,256,1536]{2,1,0:T(8,128)(2,1)}, u32[]{:S(2)}) copy-start(bf16[1,256,1536]{2,1,0:T(8,128)(2,1)} %param.15) | copy-start | bytes 2359300
  7.2 82.1 %all-gather.10.cloned.1.call-start = ((), (), s32[]{:S(2)}) async-start(), calls=%async_computation.13 | async-start | bytes 8110080 | tf_op jit(solution)/shard_map/all_gather | solution.py:92
  7.9 172.2 %all-gather.12.cloned.1.call-start = ((), (), s32[]{:S(2)}) async-start(), calls=%async_computation.14 | async-start | bytes 4866048 | tf_op jit(solution)/shard_map/all_gather | solution.py:93
  52.3 42.5 %copy-start.26 = (f32[256,64]{0,1:T(8,128)}, f32[256,64]{0,1:T(8,128)S(1)}, u32[]{:S(2)}) copy-start(f32[256,64]{0,1:T(8,128)S(1)} %get-tuple-element.430) | copy-start | bytes 196612
  52.3 53.7 %copy-start.28 = (f32[256,64]{0,1:T(8,128)}, f32[256,64]{0,1:T(8,128)S(1)}, u32[]{:S(2)}) copy-start(f32[256,64]{0,1:T(8,128)S(1)} %get-tuple-element.431) | copy-start | bytes 196612
  57.0 37.8 %copy-start.36 = (f32[1536]{0:T(1024)}, f32[1536]{0:T(1024)S(1)}, u32[]{:S(2)}) copy-start(f32[1536]{0:T(1024)S(1)} %get-tuple-element.365) | copy-start | bytes 18436
  57.0 140.0 %copy-start.42 = (f32[1536]{0:T(1024)}, f32[1536]{0:T(1024)S(1)}, u32[]{:S(2)}) copy-start(f32[1536]{0:T(1024)S(1)} %get-tuple-element.364) | copy-start | bytes 18436
  57.2 37.6 %copy-start.54 = (f32[256]{0:T(256)}, f32[256]{0:T(256)S(1)}, u32[]{:S(2)}) copy-start(f32[256]{0:T(256)S(1)} %fusion.69) | copy-start | bytes 3076
  108.1 9.4 all-to-all-start.1
  117.5 8.8 all-to-all-start.2
  126.2 17.9 all-to-all-start
  129.7 122.4 %all-gather.22.cloned.1.call-start = ((), (), s32[]{:S(2)}) async-start(), calls=%async_computation.23 | async-start | bytes 3932160 | tf_op jit(solution)/shard_map/all_gather | solution.py:183
  176.5 15.7 all-to-all-start.3
  180.0 94.7 %all-gather.14.cloned.1.call-start = ((), (), s32[]{:S(2)}) async-start(), calls=%async_computation.15 | async-start | bytes 3932160 | tf_op jit(solution)/shard_map/all_gather | solution.py:153
  198.7 196.6 %all-gather.16.cloned.1.call-start = ((), (), s32[]{:S(2)}) async-start(), calls=%async_computation.16 | async-start | bytes 17694720 | tf_op jit(solution)/shard_map/all_gather | solution.py:165
  199.3 338.2 %all-gather.18.cloned.1.call-start = ((), (), s32[]{:S(2)}) async-start(), calls=%async_computation.17 | async-start | bytes 17694720 | tf_op jit(solution)/shard_map/all_gather | solution.py:166
  199.8 480.0 %all-gather.20.cloned.1.call-start = ((), (), s32[]{:S(2)}) async-start(), calls=%async_computation.18 | async-start | bytes 17694720 | tf_op jit(solution)/shard_map/all_gather | solution.py:167
  200.6 691.3 %reduce-scatter.10.cloned.1.call-start = ((), (), s32[]{:S(2)}) async-start(), calls=%async_computation.20 | async-start | bytes 7864320 | tf_op jit(solution)/shard_map/reduce_scatter | solution.py:211
  204.4 47.2 %copy-start.60 = (s32[2]{0:T(128)S(1)}, s32[2]{0:T(128)}, u32[]{:S(2)}) copy-start(s32[2]{0:T(128)} %constant.133) | copy-start | bytes 28
  204.4 47.3 %copy-start.59 = (s32[2]{0:T(128)S(1)}, s32[2]{0:T(128)}, u32[]{:S(2)}) copy-start(s32[2]{0:T(128)} %constant.136) | copy-start | bytes 28
  204.4 47.6 %copy-start.30 = (f32[1,1024,8]{1,2,0:T(8,128)S(1)}, f32[1,1024,8]{1,2,0:T(8,128)}, u32[]{:S(2)}) copy-start(f32[1,1024,8]{1,2,0:T(8,128)} %param.22) | copy-start | bytes 98308
  552.6 142.8 %copy-start.5 = (bf16[10,205,512]{2,1,0:T(8,128)(2,1)}, bf16[10,205,512]{2,1,0:T(8,128)(2,1)S(1)}, u32[]{:S(2)}) copy-start(bf16[10,205,512]{2,1,0:T(8,128)(2,1)S(1)} %get-tuple-element.425) | copy-start | bytes 6297604
  732.5 90.9 %copy-start.40 = (f32[10,205]{1,0:T(8,128)}, f32[10,205]{1,0:T(8,128)S(1)}, u32[]{:S(2)}) copy-start(f32[10,205]{1,0:T(8,128)S(1)} %reshape.321) | copy-start | bytes 24604
  823.3 116.2 %reduce-scatter.8.cloned.1.call-start = ((), (), s32[]{:S(2)}) async-start(), calls=%async_computation.19 | async-start | bytes 3932160 | tf_op jit(solution)/shard_map/reduce_scatter | solution.py:179
  881.1 58.4 %copy-start.20 = (bf16[1,256,1536]{2,1,0:T(8,128)(2,1)S(1)}, bf16[1,256,1536]{2,1,0:T(8,128)(2,1)}, u32[]{:S(2)}) copy-start(bf16[1,256,1536]{2,1,0:T(8,128)(2,1)} %param.25) | copy-start | bytes 2359300
  948.6 14.7 all-to-all-start.4
  1023.7 14.7 all-to-all-start.6
  1038.4 14.0 all-to-all-start.5
  1052.4 8.8 all-to-all-start.7
  1055.8 300.0 %reduce-scatter.12.cloned.1.call-start = ((), (), s32[]{:S(2)}) async-start(), calls=%async_computation.21 | async-start | bytes 26763264 | tf_op jit(solution)/shard_map/reduce_scatter | solution.py:299
  1103.8 707.6 %reduce-scatter.16.cloned.1.call-start = ((), (), s32[]{:S(2)}) async-start(), calls=%async_computation.24 | async-start | bytes 53084160
  1238.4 608.5 %reduce-scatter.14.cloned.1.call-start = ((), (), s32[]{:S(2)}) async-start(), calls=%async_computation.22 | async-start | bytes 40960 | tf_op jit(solution)/shard_map/reduce_scatter | solution.py:212
  (64 other events, 564.6 us)
Sparse Core Ops, SparseCore 0:
  11.0 78.1 all-gather.9
  92.3 64.7 all-gather.11
  158.9 46.2 all-gather.21
  207.5 43.7 all-gather.13
  252.7 142.5 all-gather.15
  396.7 140.6 all-gather.17
  539.1 140.6 all-gather.19
  823.4 68.4 reduce-scatter.9
  895.5 43.9 reduce-scatter.7
  1103.9 251.8 reduce-scatter.11
  1358.1 453.1 reduce-scatter.15
  1814.5 21.9 reduce-scatter.13
where the time goes:
time: 1860 us; the launch traced here: 1850 us
  waiting for transfers between devices  1070 us (58%)
  local copies, waits for them, and re-layouts  315 us (17%)
  matrix products  216 us (12%)
  other arithmetic  165 us (9%)
  blocking collectives  43.3 us (2%)
  starting transfers between devices  29.8 us (2%)
    unnamed x13, waiting for transfers between devices  454 us
    unnamed x131, local copies, waits for them, and re-layouts  131 us
    all_gather x1, waiting for transfers between devices, local(): lax.all_gather(expert_up, 'fsdp', axis=0, tiled=True)  129 us
    all_gather x1, waiting for transfers between devices, local(): lax.all_gather(expert_down, 'fsdp', axis=0, tiled=True)  127 us
    reduce_scatter x1, waiting for transfers between devices, local(): lax.psum_scatter(jnp.concatenate([mixing_term, output_term, gains_term],...  113 us
    all_gather x1, waiting for transfers between devices, local(): lax.all_gather(expert_gate, 'fsdp', axis=0, tiled=True)  101 us
    reduce_scatter x1, waiting for transfers between devices, local(): lax.psum_scatter(partial_sum.astype(jnp.bfloat16), 'seq', scatter_dimensi...  45.2 us
    all_gather x1, blocking collectives, local(): lax.all_gather(norm_gains, ('seq', 'fsdp'), axis=0, tiled=True)  43.3 us
  transfers between devices with their start and end apart: 20, of which 15 were waited for; matrix products, arithmetic and copies ran while one was open for 23% of the time, Pallas kernels for 0%

commit v1 on v0

--- a/solution.py
+++ b/solution.py
@@ -14,6 +14,22 @@
 QBLK = 512
 epsilon = 1e-05
 rope_base = 10000.0
+
+
+def load_blocks(local_values):
+    axis_n = lax.axis_size("fsdp")
+    steps_seen = list(map(lambda i0: (i0, (i0 + 1) % axis_n), range(axis_n)))
+    pile = list(map(lambda i0: (i0, (i0 - 1) % axis_n), range(axis_n)))
+    answer, built = ([local_values], [local_values])
+    for _ in range(axis_n // 2):
+        answer.append(lax.ppermute(answer[-1], "fsdp", steps_seen))
+    for _ in range((axis_n - 1) // 2):
+        built.append(lax.ppermute(built[-1], "fsdp", pile))
+    return jnp.roll(
+        jnp.concatenate([*answer[::-1], *built[1:]], axis=0),
+        (lax.axis_index("fsdp") - axis_n // 2) * local_values.shape[0],
+        axis=0,
+    )
 
 
 def norm_apply(values, gain_row):
@@ -162,7 +178,7 @@
     padded_rows = jnp.concatenate([seq_rows, jnp.zeros((1, D), narrow)], 0)
     slot_rows = padded_rows[slot_table]
     gate_full, up_full, down_full = (
-        lax.all_gather(expert_gate, "fsdp", axis=0, tiled=True),
+        load_blocks(expert_gate),
         lax.all_gather(expert_up, "fsdp", axis=0, tiled=True),
         lax.all_gather(expert_down, "fsdp", axis=0, tiled=True),
     )

time: 1860 us -> 1880 us (1.011)
  local copies, waits for them, and re-layouts: 315 us -> 357 us
  waiting for transfers between devices: 1070 us -> 1030 us
    ppermute x0 -> x7, waiting for transfers between devices: none -> 176 us  [the longest x4 149 us: load_blocks(): answer.append(lax.ppermute(answer[-1], 'fsdp', steps_seen))]
    all_gather x1, waiting for transfers between devices: 129 us -> 0.01 us  [local(): lax.all_gather(expert_up, 'fsdp', axis=0, tiled=True)]
    all_gather x1, waiting for transfers between devices: 127 us -> 73.5 us  [local(): lax.all_gather(expert_down, 'fsdp', axis=0, tiled=True)]
    unnamed x131 -> x154, local copies, waits for them, and re-layouts: 131 us -> 171 us
    all_gather x1, waiting for transfers between devices: 101 us -> 70.6 us  [local(): lax.all_gather(expert_gate, 'fsdp', axis=0, tiled=True)]
  transfers between devices with their start and end apart: 20 -> 27, of which waited for: 15 -> 20; matrix products, arithmetic and copies ran while one was open for 23% -> 29% of each run, Pallas kernels for 0% -> 0%
where the time goes in v1:
time: 1880 us; the launch traced here: 1870 us
  waiting for transfers between devices  1030 us (55%)
  local copies, waits for them, and re-layouts  357 us (19%)
  matrix products  218 us (12%)
  other arithmetic  165 us (9%)
  blocking collectives  43.3 us (2%)
  starting transfers between devices  41 us (2%)
    unnamed x13, waiting for transfers between devices  454 us
    unnamed x154, local copies, waits for them, and re-layouts  171 us
    ppermute x4, waiting for transfers between devices, load_blocks(): answer.append(lax.ppermute(answer[-1], 'fsdp', steps_seen))  149 us
    reduce_scatter x1, waiting for transfers between devices, local(): lax.psum_scatter(jnp.concatenate([mixing_term, output_term, gains_term],...  113 us
    all_gather x1, waiting for transfers between devices, local(): lax.all_gather(expert_down, 'fsdp', axis=0, tiled=True)  73.5 us
    all_gather x1, waiting for transfers between devices, local(): lax.all_gather(expert_gate, 'fsdp', axis=0, tiled=True)  70.6 us
    reduce_scatter x1, waiting for transfers between devices, local(): lax.psum_scatter(partial_sum.astype(jnp.bfloat16), 'seq', scatter_dimensi...  45.2 us
    all_gather x1, blocking collectives, local(): lax.all_gather(norm_gains, ('seq', 'fsdp'), axis=0, tiled=True)  43.3 us
  transfers between devices with their start and end apart: 27, of which 20 were waited for; matrix products, arithmetic and copies ran while one was open for 29% of the time, Pallas kernels for 0%

profile of v1, /device:TPU:0, one launch (start us, length us, event | category | flops | bytes accessed | tf_op | source)
XLA Modules:
  0.0 1871.8 jit_solution(142029690949257419)
XLA Ops:
  8.7 43.3 %all-gather.1 = bf16[32,48,2]{1,2,0:T(2,128)(2,1)S(1)} all-gather(bf16[1,48,2]{1,2,0:T(2,128)(2,1)} %bitcast.351), channel_id=1, replica_groups=mesh['seq'=4,'fsdp'=8] {'seq','fsdp'}, dimensions={0}, use_global_device_ids=true | all-gather | bytes 6336 | tf_op jit(solution)/shard_map/all_gather | solution.py:110
  57.3 32.0 %all-gather.10.cloned.1.call-done = bf16[1536,2560]{1,0:T(8,128)(2,1)} async-done(((bf16[48,2560]{1,0:T(8,128)(2,1)}), bf16[1536,2560]{1,0:T(8,128)(2,1)}) %all-gather.10.cloned.1.call-update) | async-done | bytes 7864336 | tf_op jit(solution)/shard_map/all_gather | solution.py:108
  131.2 12.9 all-to-all-done
  147.5 23.8 %while.28 = (s32[]{:T(128)}, bf16[2,512,2,3,64]{1,4,3,2,0:T(8,128)(2,1)S(1)}, f32[2,2,3,512]{3,2,1,0:T(4,128)S(1)}, s32[2]{0:T(128)S(1)}, bf16[2,512,2,3,64]{1,4...) while((s32[]{:T(128)}, ...), condition=%wide.region_4.5_spmd.clone, body=%wide.region_1.4_spmd.clone.sunk | while | flops 843773440 | bytes 41279608 | solution.py:160
  201.5 25.8 %collective-permute-done = bf16[192,10,512]{2,0,1:T(8,128)(2,1)S(1)} collective-permute-done((bf16[192,10,512]{2,0,1:T(8,128)(2,1)S(1)}, bf16[192,10,512]{2,0,1:T(8,128)(2,1)S(1)}, u32[]{:S(2)}, u32[]{:S(2)}) %collective-permute-start) | collective-permute-done | bytes 1966112 | tf_op jit(solution)/shard_map/ppermute | solution.py:25
  230.9 50.2 %collective-permute-done.1 = bf16[192,10,512]{2,0,1:T(8,128)(2,1)} collective-permute-done((bf16[192,10,512]{2,0,1:T(8,128)(2,1)S(1)}, bf16[192,10,512]{2,0,1:T(8,128)(2,1)}, u32[]{:S(2)}, u32[]{:S(2)}) %collective-permute-start.1) | collective-permute-done | bytes 1966112 | tf_op jit(solution)/shard_map/ppermute | solution.py:25
  299.1 70.2 %collective-permute-done.2 = bf16[192,10,512]{2,0,1:T(8,128)(2,1)} collective-permute-done((bf16[192,10,512]{2,0,1:T(8,128)(2,1)}, bf16[192,10,512]{2,0,1:T(8,128)(2,1)}, u32[]{:S(2)}, u32[]{:S(2)}) %collective-permute-start.2) | collective-permute-done | bytes 1966112 | tf_op jit(solution)/shard_map/ppermute | solution.py:25
  371.1 37.9 %scatter_custom_fusion.3 = s32[2060]{0:T(1024)S(1)} fusion(s32[10240]{0:T(1024)S(1)} %reshape.356, s32[10240]{0:T(1024)S(1)} %reshape.358, s32[]{:T(128)} %constant.70.clone.1), kind=kCustom, calls=%fused_computation.197 | custom fusion | bytes 8244
  455.5 23.7 %collective-permute-done.6 = bf16[192,10,512]{2,0,1:T(8,128)(2,1)} collective-permute-done((bf16[192,10,512]{2,0,1:T(8,128)(2,1)}, bf16[192,10,512]{2,0,1:T(8,128)(2,1)}, u32[]{:S(2)}, u32[]{:S(2)}) %collective-permute-start.6) | collective-permute-done | bytes 1966112 | tf_op jit(solution)/shard_map/ppermute | solution.py:27
  522.8 13.2 fusion.57
  536.0 14.4 multiply_convert_fusion.3
  550.4 73.5 %all-gather.18.cloned.1.call-done = bf16[1536,10,512]{2,0,1:T(8,128)(2,1)} async-done(((bf16[192,10,512]{2,0,1:T(8,128)(2,1)}), bf16[1536,10,512]{2,0,1:T(8,128)(2,1)}) %all-gather.18.cloned.1.call-update) | async-done | bytes 15728656 | tf_op jit(solution)/shard_map/all_gather | solution.py:183
  623.9 18.0 multiply_reduce_fusion
  642.0 16.0 scatter_custom_fusion.4
  659.1 20.2 %gather_fusion.2 = f32[2050]{0:T(1024)S(1)} fusion(f32[1025,10]{1,0:T(8,128)S(1)} %concatenate.51, s32[2050]{0:T(1024)S(1)} %reshape.318), kind=kCustom, calls=%fused_computation.2 | custom fusion | bytes 32800 | tf_op jit(solution)/shard_map/gather | solution.py:177
  679.4 16.2 multiply_convert_fusion.1
  695.6 70.6 %all-gather.20.cloned.1.call-done = bf16[1536,10,512]{2,0,1:T(8,128)(2,1)} async-done(((bf16[192,10,512]{2,0,1:T(8,128)(2,1)}), bf16[1536,10,512]{2,0,1:T(8,128)(2,1)}) %all-gather.20.cloned.1.call-update) | async-done | bytes 15728656 | tf_op jit(solution)/shard_map/all_gather | solution.py:205
  777.3 16.0 convolution_add_fusion
  793.3 12.4 reshape.352
  805.7 29.5 %scatter_custom_fusion.2 = f32[1025,1536]{1,0:T(8,128)} fusion(s32[2050]{0:T(1024)} %copy-done.52, f32[2050,1536]{1,0:T(8,128)} %reshape.352, f32[]{:T(128)} %constant.57.clone.1), kind=kCustom, calls=%fused_computation.89 | custom fusion | flops 3148800 | bytes 6298112 | tf_op jit(solution)/shard_map/scatter-add | solution.py:218
  851.3 13.2 reshape.344
  864.5 29.3 %scatter_custom_fusion.1 = f32[1025,1536]{1,0:T(8,128)} fusion(s32[2050]{0:T(1024)} %copy-done.52, f32[2050,1536]{1,0:T(8,128)} %reshape.344, f32[]{:T(128)} %constant.57.clone.1), kind=kCustom, calls=%fused_computation.91 | custom fusion | flops 3148800 | bytes 6298112 | tf_op jit(solution)/shard_map/scatter-add | solution.py:193
  912.0 45.2 %reduce-scatter.8.cloned.1.call-done = bf16[256,1536]{1,0:T(8,128)(2,1)} async-done(((bf16[1024,1536]{1,0:T(8,128)(2,1)}), bf16[256,1536]{1,0:T(8,128)(2,1)}) %reduce-scatter.8.cloned.1.call-update) | async-done | bytes 786448 | tf_op jit(solution)/shard_map/reduce_scatter | solution.py:195
  984.3 56.4 %while.29 = (s32[]{:T(128)}, f32[1024,2,64]{0,2,1:T(8,128)S(1)}, f32[1024,2,64]{0,2,1:T(8,128)}, bf16[2,512,2,3,64]{1,4,3,2,0:T(8,128)(2,1)}, bf16[2,512,2,3,64]...) while((s32[]{:T(128)}, f32[1024,2,64]{0,2,1:T(8,128)S(1)}, ...), condition=%wide.region_21.22_spmd.clone, body=%wide.region_19.21_spmd.clone.sunk | while | flops 2062022144 | bytes 184250800 | solution.py:273
  1093.9 27.6 %concatenate.55 = f32[1536,4098]{1,0:T(8,128)} concatenate(f32[1536,2560]{1,0:T(8,128)} %fusion.74, f32[1536,1536]{1,0:T(8,128)} %fusion.77, f32[1536,1]{1,0:T(8,128)S(1)} %stack.8, f32[1536,1]{1,0:T(8,128)S(1)} %copy-done.28), dimensions={1} | concatenate | bytes 50356224 | tf_op jit(solution)/shard_map/concatenate | solution.py:316
  1123.2 12.3 convert_bitcast_fusion.1
  1135.5 12.8 convert_bitcast_fusion.2
  1148.3 15.1 convert_bitcast_fusion
  1163.4 35.3 %pad_maximum_fusion = bf16[1536,10,1536]{0,2,1:T(8,128)(2,1)} fusion(bf16[1536,10,512]{0,2,1:T(8,128)(2,1)} %convert_bitcast_fusion, bf16[1536,10,512]{0,2,1:T(8,128)(2,1)} %convert_bitcast_fusion.1, bf16[1536,10,512]{0,2,1:T(8,128)(2,1)} %convert_bitcast_fusion.2), kind=kLoop, calls=%fused_computation.74 | loop fusion | flops 141557760 | bytes 94371840 | tf_op jit(solution)/shard_map/concatenate | solution.py:234
  1198.7 57.4 %copy.314 = bf16[1536,15360]{1,0:T(8,128)(2,1)} copy(bf16[1536,15360]{0,1:T(8,128)(2,1)} %bitcast.319) | data formatting | bytes 94371840
  1260.7 112.8 %reduce-scatter.12.cloned.1.call-done = f32[48,4098]{1,0:T(8,128)} async-done(((f32[1536,4098]{1,0:T(8,128)}), f32[48,4098]{1,0:T(8,128)}) %reduce-scatter.12.cloned.1.call-update) | async-done | bytes 786832 | tf_op jit(solution)/shard_map/reduce_scatter | solution.py:315
  1378.4 450.7 %reduce-scatter.16.cloned.1.call-done = bf16[192,15360]{1,0:T(8,128)(2,1)} async-done(((bf16[1536,15360]{1,0:T(8,128)(2,1)}), bf16[192,15360]{1,0:T(8,128)(2,1)}) %reduce-scatter.16.cloned.1.call-update) | async-done | bytes 5898256
  (416 shorter events, 447.9 us)
Async XLA Ops:
  7.2 82.1 %all-gather.10.cloned.1.call-start = ((), (), s32[]{:S(2)}) async-start(), calls=%async_computation.13 | async-start | bytes 8110080 | tf_op jit(solution)/shard_map/all_gather | solution.py:108
  7.9 172.3 %all-gather.12.cloned.1.call-start = ((), (), s32[]{:S(2)}) async-start(), calls=%async_computation.14 | async-start | bytes 4866048 | tf_op jit(solution)/shard_map/all_gather | solution.py:109
  57.0 140.3 %copy-start.45 = (f32[1536]{0:T(1024)}, f32[1536]{0:T(1024)S(1)}, u32[]{:S(2)}) copy-start(f32[1536]{0:T(1024)S(1)} %get-tuple-element.364) | copy-start | bytes 18436
  108.1 9.4 all-to-all-start.1
  117.5 8.8 all-to-all-start.2
  126.2 17.9 all-to-all-start
  129.7 283.6 %all-gather.22.cloned.1.call-start = ((), (), s32[]{:S(2)}) async-start(), calls=%async_computation.23 | async-start | bytes 3932160 | tf_op jit(solution)/shard_map/all_gather | solution.py:199
  176.6 15.8 all-to-all-start.3
  180.1 323.1 %all-gather.14.cloned.1.call-start = ((), (), s32[]{:S(2)}) async-start(), calls=%async_computation.15 | async-start | bytes 3932160 | tf_op jit(solution)/shard_map/all_gather | solution.py:169
  199.5 336.6 %all-gather.16.cloned.1.call-start = ((), (), s32[]{:S(2)}) async-start(), calls=%async_computation.16 | async-start | bytes 17694720 | tf_op jit(solution)/shard_map/all_gather | solution.py:182
  200.1 423.8 %all-gather.18.cloned.1.call-start = ((), (), s32[]{:S(2)}) async-start(), calls=%async_computation.17 | async-start | bytes 17694720 | tf_op jit(solution)/shard_map/all_gather | solution.py:183
  200.6 565.6 %all-gather.20.cloned.1.call-start = ((), (), s32[]{:S(2)}) async-start(), calls=%async_computation.19 | async-start | bytes 17694720 | tf_op jit(solution)/shard_map/all_gather | solution.py:205
  201.4 708.2 %reduce-scatter.10.cloned.1.call-start = ((), (), s32[]{:S(2)}) async-start(), calls=%async_computation.20 | async-start | bytes 7864320 | tf_op jit(solution)/shard_map/reduce_scatter | solution.py:227
  201.4 25.9 %collective-permute-start = (bf16[192,10,512]{2,0,1:T(8,128)(2,1)S(1)}, bf16[192,10,512]{2,0,1:T(8,128)(2,1)S(1)}, u32[]{:S(2)}, u32[]{:S(2)}) collective-permute-start(bf16[192,10,512]{2,0,1:T(8,128)(2,1)S(1)} %copy-done.7), channel_id=1, source_target_pairs={{0,1},{1,2},{2,3},{3,4},{4,5},{5,6},{6,7},{7,0},{8,9},{9,10},{10,1... | collective-permute-start | bytes 5898248 | tf_op jit(solution)/shard_map/ppermute | solution.py:25
  227.4 53.7 %collective-permute-start.1 = (bf16[192,10,512]{2,0,1:T(8,128)(2,1)S(1)}, bf16[192,10,512]{2,0,1:T(8,128)(2,1)}, u32[]{:S(2)}, u32[]{:S(2)}) collective-permute-start(bf16[192,10,512]{2,0,1:T(8,128)(2,1)S(1)} %collective-permute-done), channel_id=1, source_target_pairs={{0,1},{1,2},{2,3},{3,4},{4,5},{5,6},{6,7},{7,0},{8,9},{9,10},{10,1... | collective-permute-start | bytes 5898248 | tf_op jit(solution)/shard_map/ppermute | solution.py:25
  227.4 57.2 %collective-permute-start.4 = (bf16[192,10,512]{2,0,1:T(8,128)(2,1)S(1)}, bf16[192,10,512]{2,0,1:T(8,128)(2,1)}, u32[]{:S(2)}, u32[]{:S(2)}) collective-permute-start(bf16[192,10,512]{2,0,1:T(8,128)(2,1)S(1)} %copy-done.7), channel_id=1, source_target_pairs={{0,7},{1,0},{2,1},{3,2},{4,3},{5,4},{6,5},{7,6},{8,15},{9,8},{10,9... | collective-permute-start | bytes 5898248 | tf_op jit(solution)/shard_map/ppermute | solution.py:27
  281.1 88.2 %collective-permute-start.2 = (bf16[192,10,512]{2,0,1:T(8,128)(2,1)}, bf16[192,10,512]{2,0,1:T(8,128)(2,1)}, u32[]{:S(2)}, u32[]{:S(2)}) collective-permute-start(bf16[192,10,512]{2,0,1:T(8,128)(2,1)} %collective-permute-done.1), channel_id=1, source_target_pairs={{0,1},{1,2},{2,3},{3,4},{4,5},{5,6},{6,7},{7,0},{8,9},{9,10},{10,1... | collective-permute-start | bytes 5898248 | tf_op jit(solution)/shard_map/ppermute | solution.py:25
  284.6 124.8 %collective-permute-start.5 = (bf16[192,10,512]{2,0,1:T(8,128)(2,1)}, bf16[192,10,512]{2,0,1:T(8,128)(2,1)}, u32[]{:S(2)}, u32[]{:S(2)}) collective-permute-start(bf16[192,10,512]{2,0,1:T(8,128)(2,1)} %collective-permute-done.4), channel_id=1, source_target_pairs={{0,7},{1,0},{2,1},{3,2},{4,3},{5,4},{6,5},{7,6},{8,15},{9,8},{10,9... | collective-permute-start | bytes 5898248 | tf_op jit(solution)/shard_map/ppermute | solution.py:27
  291.8 117.4 %copy-start.64 = (s32[2]{0:T(128)S(1)}, s32[2]{0:T(128)}, u32[]{:S(2)}) copy-start(s32[2]{0:T(128)} %constant.159) | copy-start | bytes 28
  291.8 117.5 %copy-start.63 = (s32[2]{0:T(128)S(1)}, s32[2]{0:T(128)}, u32[]{:S(2)}) copy-start(s32[2]{0:T(128)} %constant.162) | copy-start | bytes 28
  291.8 121.4 %copy-start.33 = (f32[1,1024,8]{1,2,0:T(8,128)S(1)}, f32[1,1024,8]{1,2,0:T(8,128)}, u32[]{:S(2)}) copy-start(f32[1,1024,8]{1,2,0:T(8,128)} %param.22) | copy-start | bytes 98308
  369.3 68.3 %collective-permute-start.3 = (bf16[192,10,512]{2,0,1:T(8,128)(2,1)}, bf16[192,10,512]{2,0,1:T(8,128)(2,1)}, u32[]{:S(2)}, u32[]{:S(2)}) collective-permute-start(bf16[192,10,512]{2,0,1:T(8,128)(2,1)} %collective-permute-done.2), channel_id=1, source_target_pairs={{0,1},{1,2},{2,3},{3,4},{4,5},{5,6},{6,7},{7,0},{8,9},{9,10},{10,1... | collective-permute-start | bytes 5898248 | tf_op jit(solution)/shard_map/ppermute | solution.py:25
  409.4 69.8 %collective-permute-start.6 = (bf16[192,10,512]{2,0,1:T(8,128)(2,1)}, bf16[192,10,512]{2,0,1:T(8,128)(2,1)}, u32[]{:S(2)}, u32[]{:S(2)}) collective-permute-start(bf16[192,10,512]{2,0,1:T(8,128)(2,1)} %collective-permute-done.5), channel_id=1, source_target_pairs={{0,7},{1,0},{2,1},{3,2},{4,3},{5,4},{6,5},{7,6},{8,15},{9,8},{10,9... | collective-permute-start | bytes 5898248 | tf_op jit(solution)/shard_map/ppermute | solution.py:27
  679.4 161.7 %copy-start.43 = (f32[10,205]{1,0:T(8,128)}, f32[10,205]{1,0:T(8,128)S(1)}, u32[]{:S(2)}) copy-start(f32[10,205]{1,0:T(8,128)S(1)} %reshape.321) | copy-start | bytes 24604
  841.0 116.1 %reduce-scatter.8.cloned.1.call-start = ((), (), s32[]{:S(2)}) async-start(), calls=%async_computation.18 | async-start | bytes 3932160 | tf_op jit(solution)/shard_map/reduce_scatter | solution.py:195
  966.2 15.0 all-to-all-start.4
  1041.6 14.6 all-to-all-start.6
  1056.2 14.0 all-to-all-start.5
  1070.2 8.8 all-to-all-start.7
  1073.6 299.9 %reduce-scatter.12.cloned.1.call-start = ((), (), s32[]{:S(2)}) async-start(), calls=%async_computation.21 | async-start | bytes 26763264 | tf_op jit(solution)/shard_map/reduce_scatter | solution.py:315
  1121.6 707.6 %reduce-scatter.16.cloned.1.call-start = ((), (), s32[]{:S(2)}) async-start(), calls=%async_computation.24 | async-start | bytes 53084160
  1256.2 608.5 %reduce-scatter.14.cloned.1.call-start = ((), (), s32[]{:S(2)}) async-start(), calls=%async_computation.22 | async-start | bytes 40960 | tf_op jit(solution)/shard_map/reduce_scatter | solution.py:228
  (75 other events, 1516.5 us)
Sparse Core Ops, SparseCore 0:
  11.0 78.1 all-gather.9
  92.3 64.6 all-gather.11
  158.9 46.3 all-gather.21
  207.5 43.6 all-gather.13
  252.7 226.2 all-gather.15
  480.5 143.3 all-gather.17
  625.5 140.6 all-gather.19
  841.2 68.4 reduce-scatter.9
  913.2 43.9 reduce-scatter.7
  1121.7 251.7 reduce-scatter.11
  1375.9 453.2 reduce-scatter.15
  1832.3 21.9 reduce-scatter.13
